TPU v7x, 256 devices: a whole 4x4x8 slice. The times are simulated.
256 devices in a mesh: trow: 4 (over y), tcol: 4 (over x), pix: 16 (over z, core).
Axes of the slice: x: 4, y: 4, z: 8, core: 2. Of those that a mesh axis runs over, the one named last changes fastest.
Arguments:
- frames: float32 [6144, 2, 64, 128], P(('trow', 'tcol'), None, 'pix'), may hold values from 0.1 to 8
- drift: int32 [6144, 2], P(('trow', 'tcol')), may hold values from -7 to 7
Outputs:
- inner_cycle: float32 [6144, 6144], P(('trow', 'pix'), 'tcol')
- second_band_twotime: float32 [6144, 6144], P(('trow', 'pix'), 'tcol')
All inputs are finite; a program needn't handle non-finite values.
Results may differ from a plain program's by a relative error of at most 0.0003.
Values may be sent and summed in bfloat16 or wider, within the bound.
A program may use at most 128 MiB of HBM per device.

v0:
```python
import jax
import jax.numpy as jnp
from jax import lax
from jax.sharding import PartitionSpec as P


def extended(cells, sides, width):
    for axis, dim in sides:
        count = lax.axis_size(axis)
        ends = count - 1
        head = lax.slice_in_dim(cells, 0, width, axis=dim)
        tail = lax.slice_in_dim(cells, cells.shape[dim] - width, cells.shape[dim], axis=dim)
        cells = jnp.concatenate(
            [
                lax.ppermute(tail, axis, [(i, (i + 1) % count) for i in range(ends)]),
                cells,
                lax.ppermute(head, axis, [((i + 1) % count, i) for i in range(ends)]),
            ],
            axis=dim,
        )
    return cells


def blend(padded, steps, device_axis):
    upward = (jnp.maximum(steps, 0).astype(jnp.float32) / 8.0)[:, None, None, None]
    downward = (jnp.maximum(-steps, 0).astype(jnp.float32) / 8.0)[:, None, None, None]
    length = padded.shape[device_axis] - 2
    middle = lax.slice_in_dim(padded, 1, 1 + length, 1, device_axis)
    after = lax.slice_in_dim(padded, 2, 2 + length, 1, device_axis)
    before = lax.slice_in_dim(padded, 0, length, 1, device_axis)
    return (1.0 - upward - downward) * middle + upward * after + downward * before


def per_device(frames, drift):
    local_frames = frames.shape[0]
    tile_rows = frames.shape[2]
    columns = frames.shape[3]
    total_frames = local_frames * lax.axis_size("trow") * lax.axis_size("tcol")
    band_pixels = tile_rows * columns * lax.axis_size("pix")
    padded = extended(frames.astype(jnp.bfloat16), (("pix", 2),), 1).astype(frames.dtype)
    rowpass = blend(padded, drift[:, 0], 2)
    padded = jnp.pad(rowpass, ((0, 0), (0, 0), (0, 0), (1, 1)))
    shifted = blend(padded, drift[:, 1], 3)
    pixel_mean = lax.psum(jnp.sum(shifted, axis=0), ("trow", "tcol")) / total_frames
    flat = shifted / pixel_mean[None]
    frame_mean = lax.psum(jnp.sum(flat, axis=(2, 3)), "pix") / band_pixels
    normed = (flat / frame_mean[:, :, None, None]).astype(jnp.bfloat16)
    normed = normed.reshape(local_frames, 2, tile_rows * columns)
    block_size = local_frames * lax.axis_size("tcol")
    everything = lax.all_gather(normed, ("trow", "tcol"), axis=0, tiled=True)
    row_frames = lax.dynamic_slice_in_dim(
        everything, lax.axis_index("trow") * block_size, block_size, 0
    )
    col_frames = lax.dynamic_slice_in_dim(
        everything, lax.axis_index("tcol") * block_size, block_size, 0
    )
    own_rows = block_size // lax.axis_size("pix")
    results = []
    for band in range(2):
        band_rows = row_frames[:, band]
        band_cols = col_frames[:, band]

        def partial_gram(start, count, band_rows=band_rows, band_cols=band_cols):
            return lax.dot_general(
                band_rows, band_cols, (((1,), (1,)), ((), ())), preferred_element_type=jnp.float32
            )

        summed = lax.psum_scatter(
            partial_gram(jnp.int32(0), lax.axis_size("pix") * own_rows),
            "pix",
            scatter_dimension=0,
            tiled=True,
        )
        results.append(summed / band_pixels)
    return (results[0], results[1])


def solution(mesh):
    in_specs = (P(("trow", "tcol"), None, "pix", None), P(("trow", "tcol"), None))
    out_specs = (P(("trow", "pix"), "tcol"), P(("trow", "pix"), "tcol"))
    return jax.shard_map(
        per_device, mesh=mesh, in_specs=in_specs, out_specs=out_specs, check_vma=False
    )
```

profile of v0, /device:TPU:6, one launch (start us, length us, event | category | flops | bytes accessed | tf_op | source)
XLA Modules:
  0.0 343.2 jit_solution(5031230959455782191)
XLA Ops:
  7.2 0.0 copy-start
  7.2 0.0 all-gather.2.cloned.1.call-start
  7.2 1.7 copy.10
  9.0 1.8 collective-permute-start
  10.7 1.3 collective-permute-start.1
  12.0 0.0 copy-done
  12.1 0.0 collective-permute-done
  12.1 3.7 %collective-permute-done.1 = bf16[384,2,1,128]{3,0,2,1:T(8,128)(2,1)S(1)} collective-permute-done((bf16[384,2,1,128]{3,0,2,1:T(8,128)(2,1)S(1)}, bf16[384,2,1,128]{3,0,2,1:T(8,128)(2,1)S(1)}, u32[]{:S(2)}, u32[]{:S(2)}) %collective-permute-start.1) | collective-permute-done | bytes 196640 | tf_op jit(solution)/shard_map/ppermute | solution.py:17
  15.8 0.2 maximum_convert_fusion
  15.9 0.4 fusion.6
  16.3 1.0 fusion.11
  17.4 32.7 %psum.14 = f32[2,4,128]{2,1,0:T(4,128)S(1)} all-reduce(f32[2,4,128]{2,1,0:T(4,128)S(1)} %get-tuple-element.6), channel_id=1, replica_groups=mesh['trow'=4,'tcol'=4,'pix'=16] {'trow','tcol'}, use_global_device_ids=true, to_apply=%region_1.2 | all-reduce | flops 1024 | bytes 8192 | tf_op jit(solution)/shard_map/psum | solution.py:44
  50.1 0.2 divide_reduce_fusion
  50.3 28.0 %psum.15 = f32[384,2]{0,1:T(2,128)S(1)} all-reduce(f32[384,2]{0,1:T(2,128)S(1)} %divide_reduce_fusion), channel_id=1, replica_groups=mesh['trow'=4,'tcol'=4,'pix'=16] {'pix'}, use_global_device_ids=true, to_apply=%region_3.4 | all-reduce | flops 768 | bytes 6144 | tf_op jit(solution)/shard_map/psum | solution.py:46
  78.3 1.2 copy_bitcast_fusion
  79.5 0.0 all-gather.2.cloned.1.call-update
  79.5 0.0 reduce-scatter.5.cloned.1.call-start
  79.6 99.5 %all-gather.2.cloned.1.call-done = bf16[6144,2,512]{2,0,1:T(8,128)(2,1)} async-done(((bf16[384,2,512]{2,0,1:T(8,128)(2,1)}), bf16[6144,2,512]{2,0,1:T(8,128)(2,1)}) %all-gather.2.cloned.1.call-update) | async-done | bytes 12582928 | tf_op jit(solution)/shard_map/all_gather | solution.py:50
  179.1 8.2 %fusion.4 = f32[1536,1536]{1,0:T(8,128)} fusion(bf16[6144,2,512]{2,0,1:T(8,128)(2,1)} %all-gather.2.cloned.1.call-done, s32[]{:T(128)S(6)} %select_n.7, s32[]{:T(128)S(6)} %add.38, s32[]{:T(128)S(6)} %select_n.6), kind=kOutput, calls=%fused_computation.7 | convolution fusion | flops 2415919104 | bytes 12584960 | tf_op jit(solution)/shard_map/dot_general | solution.py:64
  187.3 0.0 reduce-scatter.5.cloned.1.call-update
  187.3 0.0 reduce-scatter.3.cloned.1.call-start
  187.4 8.1 %fusion.5 = f32[1536,1536]{1,0:T(8,128)} fusion(bf16[6144,2,512]{2,0,1:T(8,128)(2,1)} %all-gather.2.cloned.1.call-done, s32[]{:T(128)S(6)} %select_n.7, s32[]{:T(128)S(6)} %select_n.6), kind=kOutput, calls=%fused_computation.10 | convolution fusion | flops 2415919104 | bytes 12582920 | tf_op jit(solution)/shard_map/dot_general | solution.py:64
  195.5 0.0 reduce-scatter.3.cloned.1.call-update
  195.5 64.3 %reduce-scatter.5.cloned.1.call-done = f32[96,1536]{1,0:T(8,128)} async-done(((f32[1536,1536]{1,0:T(8,128)}), f32[96,1536]{1,0:T(8,128)}) %reduce-scatter.5.cloned.1.call-update) | async-done | bytes 589840 | tf_op jit(solution)/shard_map/reduce_scatter | solution.py:68
  259.8 1.9 broadcast_multiply_fusion
  261.7 73.0 %reduce-scatter.3.cloned.1.call-done = f32[96,1536]{1,0:T(8,128)} async-done(((f32[1536,1536]{1,0:T(8,128)}), f32[96,1536]{1,0:T(8,128)}) %reduce-scatter.3.cloned.1.call-update) | async-done | bytes 589840 | tf_op jit(solution)/shard_map/reduce_scatter | solution.py:68
  334.7 1.9 broadcast_multiply_fusion.1
  (5 shorter events, 0.1 us)
Async XLA Ops:
  7.2 4.9 %copy-start = (s32[384,2]{0,1:T(2,128)S(1)}, s32[384,2]{0,1:T(2,128)}, u32[]{:S(2)}) copy-start(s32[384,2]{0,1:T(2,128)} %param.3) | copy-start | bytes 9220
  7.2 172.0 %all-gather.2.cloned.1.call-start = ((), (), s32[]{:S(2)}) async-start(), calls=%async_computation.2 | async-start | bytes 13369344 | tf_op jit(solution)/shard_map/all_gather | solution.py:50
  9.0 3.1 collective-permute-start
  10.7 5.0 %collective-permute-start.1 = (bf16[384,2,1,128]{3,0,2,1:T(8,128)(2,1)S(1)}, bf16[384,2,1,128]{3,0,2,1:T(8,128)(2,1)S(1)}, u32[]{:S(2)}, u32[]{:S(2)}) collective-permute-start(bf16[384,2,1,128]{3,0,2,1:T(8,128)(2,1)S(1)} %get-tuple-element.9), channel_id=1, source_target_pairs={{1,0},{2,1},{3,2},{4,3},{5,4},{6,5},{7,6},{8,7},{9,8},{10,9},{11,1... | collective-permute-start | bytes 589832 | tf_op jit(solution)/shard_map/ppermute | solution.py:17
  79.5 180.3 %reduce-scatter.5.cloned.1.call-start = ((), (), s32[]{:S(2)}) async-start(), calls=%async_computation.4 | async-start | bytes 10027008 | tf_op jit(solution)/shard_map/reduce_scatter | solution.py:68
  187.3 147.4 %reduce-scatter.3.cloned.1.call-start = ((), (), s32[]{:S(2)}) async-start(), calls=%async_computation.3 | async-start | bytes 10027008 | tf_op jit(solution)/shard_map/reduce_scatter | solution.py:68
Sparse Core Ops, SparseCore 0:
  79.7 99.4 all-gather.1
  187.5 72.3 reduce-scatter.4
  262.4 72.2 reduce-scatter.2
where the time goes:
time: 343 us
  waiting for transfers between devices  240 us (70%)
  blocking collectives  60.7 us (18%)
  matrix products  16.3 us (5%)
  between operations  13.8 us (4%)
  other arithmetic  6.9 us (2%)
    reduce_scatter x2, waiting for transfers between devices, per_device(): lax.psum_scatter(partial_gram(jnp.int32(0), lax.axis_size('pix') * own_ro...  137 us
    all_gather x1, waiting for transfers between devices, per_device(): everything = lax.all_gather(normed, ('trow', 'tcol'), axis=0, tiled=True)  99.5 us
    psum x1, blocking collectives, per_device(): lax.psum(jnp.sum(shifted, axis=0), ('trow', 'tcol')) / total_frames  32.7 us
    psum x1, blocking collectives, per_device(): frame_mean = lax.psum(jnp.sum(flat, axis=(2, 3)), 'pix') / band_pixels  28 us
    dot_general x2, matrix products, partial_gram(): lax.dot_general(band_rows, band_cols, (((1,), (1,)), ((), ())), preferred...  16.3 us
  transfers between devices with their start and end apart: 5, of which 4 were waited for; matrix products, arithmetic and copies ran while one was open for 3% of the time, Pallas kernels for 0%

commit v1 on v0

--- a/solution.py
+++ b/solution.py
@@ -41,7 +41,7 @@
     rowpass = blend(padded, drift[:, 0], 2)
     padded = jnp.pad(rowpass, ((0, 0), (0, 0), (0, 0), (1, 1)))
     shifted = blend(padded, drift[:, 1], 3)
-    pixel_mean = lax.psum(jnp.sum(shifted, axis=0), ("trow", "tcol")) / total_frames
+    pixel_mean = lax.psum(lax.psum(jnp.sum(shifted, axis=0), "tcol"), "trow") / total_frames
     flat = shifted / pixel_mean[None]
     frame_mean = lax.psum(jnp.sum(flat, axis=(2, 3)), "pix") / band_pixels
     normed = (flat / frame_mean[:, :, None, None]).astype(jnp.bfloat16)

time: 343 us -> 325 us (0.948)
  blocking collectives: 60.7 us -> 46.2 us
  waiting for transfers between devices: 240 us -> 236 us
    psum x1 -> x2, blocking collectives: 32.7 us -> 18.2 us  [the longest x1 10.7 us: per_device(): lax.psum(lax.psum(jnp.sum(shifted, axis=0), 'tcol'), 'trow') / total_frames]
    all_gather x1, waiting for transfers between devices: 99.5 us -> 95.2 us  [per_device(): everything = lax.all_gather(normed, ('trow', 'tcol'), axis=0, tiled=True)]
where the time goes in v1:
time: 325 us; the launch traced here: 324 us
  waiting for transfers between devices  236 us (73%)
  blocking collectives  46.2 us (14%)
  matrix products  16.3 us (5%)
  between operations  13.8 us (4%)
  other arithmetic  6.9 us (2%)
    reduce_scatter x2, waiting for transfers between devices, per_device(): lax.psum_scatter(partial_gram(jnp.int32(0), lax.axis_size('pix') * own_ro...  137 us
    all_gather x1, waiting for transfers between devices, per_device(): everything = lax.all_gather(normed, ('trow', 'tcol'), axis=0, tiled=True)  95.2 us
    psum x1, blocking collectives, per_device(): frame_mean = lax.psum(jnp.sum(flat, axis=(2, 3)), 'pix') / band_pixels  28 us
    dot_general x2, matrix products, partial_gram(): lax.dot_general(band_rows, band_cols, (((1,), (1,)), ((), ())), preferred...  16.3 us
    psum x1, blocking collectives, per_device(): lax.psum(lax.psum(jnp.sum(shifted, axis=0), 'tcol'), 'trow') / total_frames  10.7 us
    psum x1, blocking collectives, per_device(): lax.psum(jnp.sum(shifted, axis=0), 'tcol')  7.49 us
  transfers between devices with their start and end apart: 5, of which 4 were waited for; matrix products, arithmetic and copies ran while one was open for 3% of the time, Pallas kernels for 0%

profile of v1, /device:TPU:6, one launch (start us, length us, event | category | flops | bytes accessed | tf_op | source)
XLA Modules:
  0.0 324.2 jit_solution(14450483903372658085)
XLA Ops:
  7.2 0.0 copy-start
  7.2 0.0 all-gather.2.cloned.1.call-start
  7.2 1.7 copy.10
  9.0 1.8 collective-permute-start
  10.7 1.3 collective-permute-start.1
  12.0 0.0 copy-done
  12.1 0.0 collective-permute-done
  12.1 3.7 %collective-permute-done.1 = bf16[384,2,1,128]{3,0,2,1:T(8,128)(2,1)S(1)} collective-permute-done((bf16[384,2,1,128]{3,0,2,1:T(8,128)(2,1)S(1)}, bf16[384,2,1,128]{3,0,2,1:T(8,128)(2,1)S(1)}, u32[]{:S(2)}, u32[]{:S(2)}) %collective-permute-start.1) | collective-permute-done | bytes 196640 | tf_op jit(solution)/shard_map/ppermute | solution.py:17
  15.8 0.2 maximum_convert_fusion
  15.9 0.4 fusion.6
  16.3 1.0 fusion.11
  17.4 7.5 %psum.21 = f32[2,4,128]{2,1,0:T(4,128)S(1)} all-reduce(f32[2,4,128]{2,1,0:T(4,128)S(1)} %get-tuple-element.6), channel_id=1, replica_groups=mesh['trow'=4,'tcol'=4,'pix'=16] {'tcol'}, use_global_device_ids=true, to_apply=%region_1.2 | all-reduce | flops 1024 | bytes 8192 | tf_op jit(solution)/shard_map/psum | solution.py:44
  24.9 10.7 %psum.22 = f32[2,4,128]{2,1,0:T(4,128)S(1)} all-reduce(f32[2,4,128]{2,1,0:T(4,128)S(1)} %psum.21), channel_id=1, replica_groups=mesh['trow'=4,'tcol'=4,'pix'=16] {'trow'}, use_global_device_ids=true, to_apply=%region_2.3 | all-reduce | flops 1024 | bytes 8192 | tf_op jit(solution)/shard_map/psum | solution.py:44
  35.6 0.2 divide_reduce_fusion
  35.8 28.0 %psum.23 = f32[384,2]{0,1:T(2,128)S(1)} all-reduce(f32[384,2]{0,1:T(2,128)S(1)} %divide_reduce_fusion), channel_id=1, replica_groups=mesh['trow'=4,'tcol'=4,'pix'=16] {'pix'}, use_global_device_ids=true, to_apply=%region_4.5 | all-reduce | flops 768 | bytes 6144 | tf_op jit(solution)/shard_map/psum | solution.py:46
  63.8 1.2 copy_bitcast_fusion
  65.0 0.0 all-gather.2.cloned.1.call-update
  65.1 0.0 reduce-scatter.5.cloned.1.call-start
  65.1 95.2 %all-gather.2.cloned.1.call-done = bf16[6144,2,512]{2,0,1:T(8,128)(2,1)} async-done(((bf16[384,2,512]{2,0,1:T(8,128)(2,1)}), bf16[6144,2,512]{2,0,1:T(8,128)(2,1)}) %all-gather.2.cloned.1.call-update) | async-done | bytes 12582928 | tf_op jit(solution)/shard_map/all_gather | solution.py:50
  160.3 8.2 %fusion.4 = f32[1536,1536]{1,0:T(8,128)} fusion(bf16[6144,2,512]{2,0,1:T(8,128)(2,1)} %all-gather.2.cloned.1.call-done, s32[]{:T(128)S(6)} %select_n.7, s32[]{:T(128)S(6)} %add.40, s32[]{:T(128)S(6)} %select_n.6), kind=kOutput, calls=%fused_computation.7 | convolution fusion | flops 2415919104 | bytes 12584960 | tf_op jit(solution)/shard_map/dot_general | solution.py:64
  168.5 0.0 reduce-scatter.5.cloned.1.call-update
  168.5 0.0 reduce-scatter.3.cloned.1.call-start
  168.6 8.1 %fusion.5 = f32[1536,1536]{1,0:T(8,128)} fusion(bf16[6144,2,512]{2,0,1:T(8,128)(2,1)} %all-gather.2.cloned.1.call-done, s32[]{:T(128)S(6)} %select_n.7, s32[]{:T(128)S(6)} %select_n.6), kind=kOutput, calls=%fused_computation.10 | convolution fusion | flops 2415919104 | bytes 12582920 | tf_op jit(solution)/shard_map/dot_general | solution.py:64
  176.7 0.0 reduce-scatter.3.cloned.1.call-update
  176.7 64.6 %reduce-scatter.5.cloned.1.call-done = f32[96,1536]{1,0:T(8,128)} async-done(((f32[1536,1536]{1,0:T(8,128)}), f32[96,1536]{1,0:T(8,128)}) %reduce-scatter.5.cloned.1.call-update) | async-done | bytes 589840 | tf_op jit(solution)/shard_map/reduce_scatter | solution.py:68
  241.3 1.9 broadcast_multiply_fusion
  243.2 72.5 %reduce-scatter.3.cloned.1.call-done = f32[96,1536]{1,0:T(8,128)} async-done(((f32[1536,1536]{1,0:T(8,128)}), f32[96,1536]{1,0:T(8,128)}) %reduce-scatter.3.cloned.1.call-update) | async-done | bytes 589840 | tf_op jit(solution)/shard_map/reduce_scatter | solution.py:68
  315.8 1.9 broadcast_multiply_fusion.1
  (5 shorter events, 0.1 us)
Async XLA Ops:
  7.2 4.9 %copy-start = (s32[384,2]{0,1:T(2,128)S(1)}, s32[384,2]{0,1:T(2,128)}, u32[]{:S(2)}) copy-start(s32[384,2]{0,1:T(2,128)} %param.3) | copy-start | bytes 9220
  7.2 153.1 %all-gather.2.cloned.1.call-start = ((), (), s32[]{:S(2)}) async-start(), calls=%async_computation.2 | async-start | bytes 13369344 | tf_op jit(solution)/shard_map/all_gather | solution.py:50
  9.0 3.1 collective-permute-start
  10.7 5.0 %collective-permute-start.1 = (bf16[384,2,1,128]{3,0,2,1:T(8,128)(2,1)S(1)}, bf16[384,2,1,128]{3,0,2,1:T(8,128)(2,1)S(1)}, u32[]{:S(2)}, u32[]{:S(2)}) collective-permute-start(bf16[384,2,1,128]{3,0,2,1:T(8,128)(2,1)S(1)} %get-tuple-element.9), channel_id=1, source_target_pairs={{1,0},{2,1},{3,2},{4,3},{5,4},{6,5},{7,6},{8,7},{9,8},{10,9},{11,1... | collective-permute-start | bytes 589832 | tf_op jit(solution)/shard_map/ppermute | solution.py:17
  65.1 176.3 %reduce-scatter.5.cloned.1.call-start = ((), (), s32[]{:S(2)}) async-start(), calls=%async_computation.4 | async-start | bytes 10027008 | tf_op jit(solution)/shard_map/reduce_scatter | solution.py:68
  168.5 147.3 %reduce-scatter.3.cloned.1.call-start = ((), (), s32[]{:S(2)}) async-start(), calls=%async_computation.3 | async-start | bytes 10027008 | tf_op jit(solution)/shard_map/reduce_scatter | solution.py:68
Sparse Core Ops, SparseCore 0:
  65.2 95.0 all-gather.1
  168.6 72.6 reduce-scatter.4
  243.9 71.8 reduce-scatter.2
